TPU v7x, 32 devices: a whole 2x2x4 slice. The times are simulated.
32 devices in a mesh: tm: 4 (over z), tile: 8 (over y, x, core).
Axes of the slice: x: 2, y: 2, z: 4, core: 2. Of those that a mesh axis runs over, the one named last changes fastest.
Arguments:
- frames: bfloat16 [1024, 49152], P('tm', 'tile'), may hold values from -16 to 16
- segments: int32 [1024], replicated, may hold values from 0 to 2, as said below
- offset: int32 [1], replicated, may hold values from 0 to 45056
Outputs:
- instant: float32 [4096, 49152], P('tm', 'tile')
- lagged: float32 [4096, 49152], P('tm', 'tile')
Inputs may be any that keep to these rules, and one draw needn't show every extreme that they name: `segments`: each trajectory is a run of frames, in order of its id.
All inputs are finite; a program needn't handle non-finite values.
Results may differ from a plain program's by a relative error of at most 0.0036.
Values may be sent and summed in bfloat16 or wider, within the bound.
A program may use at most 128 MiB of HBM per device.

v0:
```python
import jax
import jax.numpy as jnp
from jax import lax
from jax.sharding import PartitionSpec as P

S = 4096
LAG = 256


def broadcast(value, axis, root):
    mine = lax.axis_index(axis) == root
    return lax.psum(jnp.where(mine, value, jnp.zeros_like(value)), axis)


def center(values):
    total = values.shape[0]
    mean = jnp.sum(values, axis=0, dtype=jnp.float32) / total
    return (values.astype(jnp.float32) - mean).astype(jnp.bfloat16)


def shards(frames, segments, offset):
    columns = frames.shape[1]
    tiles = lax.axis_size("tile")
    start = offset[0]
    all_columns = lax.all_gather(frames, "tm", axis=0, tiled=True)
    first = start // columns
    count = min(tiles, (S - 1) // columns + 2)
    pieces = []
    for step in range(count):
        owner = jnp.minimum(first + step, tiles - 1)
        pieces.append(broadcast(frames, "tile", owner))
    joined = jnp.concatenate(pieces, axis=1)
    local_slab = lax.dynamic_slice_in_dim(joined, start - first * columns, S, 1)
    raw_slab = lax.all_to_all(local_slab, "tm", split_axis=1, concat_axis=0, tiled=True)
    total = all_columns.shape[0]
    centered = center(all_columns)
    slab = center(raw_slab)
    dims = (((0,), (0,)), ((), ()))
    instant = lax.dot_general(slab, centered, dims, preferred_element_type=jnp.float32) / total
    span = total - LAG
    valid = (segments[:span] == segments[LAG:]).astype(jnp.bfloat16)[:, None]
    pairs = jnp.sum(valid.astype(jnp.float32))
    left = jnp.concatenate([slab[:span], slab[LAG:]], axis=0)
    right = jnp.concatenate([centered[LAG:] * valid, centered[:span] * valid], axis=0)
    lagged = lax.dot_general(left, right, dims, preferred_element_type=jnp.float32) * 0.5 / pairs
    return (instant, lagged)


def solution(mesh):
    in_specs = (P("tm", "tile"), P(), P())
    out_specs = (P("tm", "tile"), P("tm", "tile"))
    return jax.shard_map(shards, mesh=mesh, in_specs=in_specs, out_specs=out_specs, check_vma=False)
```

profile of v0, /device:TPU:0, one launch (start us, length us, event | category | flops | bytes accessed | tf_op | source)
XLA Modules:
  0.0 357.0 jit_solution(3135685952027372525)
XLA Ops:
  8.0 0.0 all-reduce.3.cloned.1.call-start
  8.7 3.2 copy.5
  11.9 3.1 broadcast_select_fusion
  15.0 0.0 all-reduce.3.cloned.1.call-update
  15.0 0.0 all-gather.2.cloned.1.call-start
  15.1 0.5 all-gather.2.cloned.1.call-update
  15.6 106.2 %all-reduce.3.cloned.1.call-done = (bf16[256,6144]{0,1:T(8,128)(2,1)}, bf16[256,6144]{0,1:T(8,128)(2,1)}) async-done(((bf16[256,6144]{0,1:T(8,128)(2,1)}, bf16[256,6144]{0,1:T(8,128)(2,1)}), (bf16[256,6144]{0,1:T(8,128)(2,1)}, bf16[256,6144]{0,1:T(8,128)(2,1)})) %all-reduce.3.cloned.1.call-update) | async-done | bytes 6291472 | tf_op jit(solution)/shard_map/psum | solution.py:12
  121.8 4.8 %fusion.11 = bf16[256,4096]{0,1:T(8,128)(2,1)} fusion(s32[]{:T(128)S(6)} %select_n.27, bf16[256,6144]{0,1:T(8,128)(2,1)} %get-tuple-element.2, bf16[256,6144]{0,1:T(8,128)(2,1)} %get-tuple-element.3), kind=kLoop, calls=%fused_computation.22 | loop fusion | flops 4194304 | bytes 8388612 | tf_op jit(solution)/shard_map/concatenate | solution.py:32
  126.6 0.0 copy-start.1
  126.6 4.7 %all-to-all-start = ((bf16[256,4,1024]{0,2,1:T(8,128)(2,1)}), bf16[256,4,1024]{0,2,1:T(8,128)(2,1)S(1)}, u32[]{:S(2)}, u32[]{:S(2)}) async-start(bf16[256,4,1024]{0,2,1:T(8,128)(2,1)} %bitcast.14), calls=%async_computation | async-start | bytes 4194304 | tf_op jit(solution)/shard_map/all_to_all | solution.py:34
  131.3 0.0 copy-done.1
  131.3 0.7 convert_reduce_fusion.2
  132.0 104.6 %all-to-all-done = bf16[256,4,1024]{0,2,1:T(8,128)(2,1)S(1)} async-done(((bf16[256,4,1024]{0,2,1:T(8,128)(2,1)}), bf16[256,4,1024]{0,2,1:T(8,128)(2,1)S(1)}, u32[]{:S(2)}, u32[]{:S(2)}) %all-to-all-start) | async-done | bytes 2097184 | tf_op jit(solution)/shard_map/all_to_all | solution.py:34
  236.6 2.4 convert_bitcast_fusion
  239.0 5.3 %copy.7 = f32[4,256,1024]{2,1,0:T(8,128)} copy(f32[4,256,1024]{1,2,0:T(8,128)} %convert_bitcast_fusion) | data formatting | bytes 8388608 | tf_op jit(solution)/shard_map/convert_element_type | solution.py:18
  244.3 0.3 convert_reduce_fusion.1
  244.6 2.8 fusion.7
  247.4 0.0 copy-start
  247.4 1.3 copy-done
  248.7 1.6 fusion.15
  250.3 32.4 %all-gather.2.cloned.1.call-done = bf16[1024,6144]{1,0:T(8,128)(2,1)} async-done(((bf16[256,6144]{1,0:T(8,128)(2,1)}), bf16[1024,6144]{1,0:T(8,128)(2,1)}) %all-gather.2.cloned.1.call-update) | async-done | bytes 12582928 | tf_op jit(solution)/shard_map/all_gather | solution.py:25
  282.7 6.4 %convert_reduce_fusion = f32[6144]{0:T(1024)S(1)} fusion(bf16[1024,6144]{1,0:T(8,128)(2,1)} %all-gather.2.cloned.1.call-done), kind=kLoop, calls=%fused_computation.1 | loop fusion | flops 12576768 | bytes 12607488 | tf_op jit(solution)/shard_map/reduce_sum | solution.py:17
  289.1 7.5 %fusion = bf16[1024,6144]{1,0:T(8,128)(2,1)S(1)} fusion(bf16[1024,6144]{1,0:T(8,128)(2,1)} %all-gather.2.cloned.1.call-done, f32[6144]{0:T(1024)S(1)} %broadcast_multiply_fusion), kind=kLoop, calls=%fused_computation.2 | loop fusion | flops 18874368 | bytes 25190400 | tf_op jit(solution)/shard_map/convert_element_type | solution.py:18
  296.6 18.3 %convolution_multiply_fusion = f32[1024,6144]{1,0:T(8,128)} fusion(bf16[1024,1024]{1,0:T(8,128)(2,1)} %copy-done, bf16[1024,6144]{1,0:T(8,128)(2,1)S(1)} %fusion), kind=kOutput, calls=%fused_computation.8 | convolution fusion | flops 12891193344 | bytes 39845888 | tf_op jit(solution)/shard_map/dot_general | solution.py:39
  315.0 6.8 %slice_multiply_fusion.1 = (bf16[768,6144]{1,0:T(8,128)(2,1)}, bf16[768,6144]{1,0:T(8,128)(2,1)}) fusion(bf16[1024,6144]{1,0:T(8,128)(2,1)S(1)} %fusion, bf16[768]{0:T(1024)(128)(2,1)S(1)} %get-tuple-element.5), kind=kLoop, calls=%fused_computation.10 | loop fusion | flops 9437184 | bytes 37750272 | tf_op jit(solution)/shard_map/mul | solution.py:44
  321.7 27.8 %multiply_divide_fusion = f32[1024,6144]{1,0:T(8,128)} fusion(f32[]{:T(128)} %get-tuple-element.4, bf16[768,6144]{1,0:T(8,128)(2,1)} %get-tuple-element.7, bf16[768,6144]{1,0:T(8,128)(2,1)} %get-tuple-element.6, bf16[768,1024]{1,0:T(8,128)(2,1)} %get-tuple-element.11, bf16[768,1024]{1,0:T(8,128)(2,1)S(1)} %get-tuple-element.10), kind=kOutput, calls=%fused_computation.3 | convolution fusion | flops 19383975936 | bytes 47185924 | tf_op jit(solution)/shard_map/dot_general | solution.py:45
  (2 shorter events, 0.0 us)
Async XLA Ops:
  8.0 113.9 %all-reduce.3.cloned.1.call-start = ((), (), s32[]{:S(2)}) async-start(), calls=%async_computation.2 | async-start | bytes 12582912 | tf_op jit(solution)/shard_map/psum | solution.py:12
  15.0 267.7 %all-gather.2.cloned.1.call-start = ((), (), s32[]{:S(2)}) async-start(), calls=%async_computation.1 | async-start | bytes 15728640 | tf_op jit(solution)/shard_map/all_gather | solution.py:25
  126.6 4.7 %copy-start.1 = (s32[1024]{0:T(1024)S(1)}, s32[1024]{0:T(1024)}, u32[]{:S(2)}) copy-start(s32[1024]{0:T(1024)} %param.4) | copy-start | bytes 12292
  126.6 110.0 %all-to-all-start = ((bf16[256,4,1024]{0,2,1:T(8,128)(2,1)}), bf16[256,4,1024]{0,2,1:T(8,128)(2,1)S(1)}, u32[]{:S(2)}, u32[]{:S(2)}) async-start(bf16[256,4,1024]{0,2,1:T(8,128)(2,1)} %bitcast.14), calls=%async_computation | async-start | bytes 4194304 | tf_op jit(solution)/shard_map/all_to_all | solution.py:34
  247.4 1.3 copy-start
Sparse Core Ops, SparseCore 0:
  15.2 106.6 all-reduce.2
Sparse Core Ops, SparseCore 1:
  17.1 265.6 all-gather.1
where the time goes:
time: 358 us; the launch traced here: 357 us
  waiting for transfers between devices  244 us (68%)
  matrix products  46.2 us (13%)
  other arithmetic  34.7 us (10%)
  between operations  16.2 us (5%)
  local copies, waits for them, and re-layouts  11.4 us (3%)
  starting transfers between devices  4.79 us (1%)
    psum x1, waiting for transfers between devices, broadcast(): return lax.psum(jnp.where(mine, value, jnp.zeros_like(value)), axis)  106 us
    all_to_all x1, waiting for transfers between devices, shards(): lax.all_to_all(local_slab, 'tm', split_axis=1, concat_axis=0, tiled=True)  105 us
    all_gather x1, waiting for transfers between devices, shards(): all_columns = lax.all_gather(frames, 'tm', axis=0, tiled=True)  32.4 us
    dot_general x1, matrix products, shards(): lax.dot_general(left, right, dims, preferred_element_type=jnp.float32) * 0.5  27.8 us
    dot_general x1, matrix products, shards(): lax.dot_general(slab, centered, dims, preferred_element_type=jnp.float32)  18.3 us
    convert_element_type x3, other arithmetic, center(): return (values.astype(jnp.float32) - mean).astype(jnp.bfloat16)  12.7 us
  transfers between devices with their start and end apart: 3, of which 3 were waited for; matrix products, arithmetic and copies ran while one was open for 5% of the time, Pallas kernels for 0%

commit v1 on v0

v1 whole, which is shorter than its diff:
```python
import functools

import jax
import jax.numpy as jnp
from jax import lax
from jax.experimental import pallas as pl
from jax.experimental.pallas import tpu as pltpu
from jax.sharding import PartitionSpec as P


S = 4096
LAG = 256
BLOCK = 256
UNITS = (7, 7, 5, 3, 2)


def chunk_kernel(total, z_ref, scale_ref, st_ref, lt_ref, own_ref, near_ref, far_ref, inner_ref, outer_ref, *rest):
    inst_ref, lag_ref, xs = rest[-3:]
    z = z_ref[0]
    rows = own_ref.shape[0]
    span = total - LAG
    inner = jnp.logical_or(z == 1, z == 2)
    last = jnp.where(inner, inner_ref[...].astype(jnp.float32), outer_ref[...].astype(jnp.float32))
    blocks = [own_ref[...].astype(jnp.float32), near_ref[...].astype(jnp.float32), far_ref[...].astype(jnp.float32), last]
    mean = sum(jnp.sum(block, axis=0, keepdims=True) for block in blocks) / total
    for k, block in enumerate(blocks):
        place = pl.multiple_of(jnp.bitwise_xor(z, k) * rows, rows)
        xs[pl.ds(place, rows), :] = (block - mean).astype(jnp.bfloat16)
    inst_ref[...] = jnp.dot(st_ref[...], xs[...], preferred_element_type=jnp.float32) / total
    lagged = jnp.dot(lt_ref[:, :span], xs[LAG:, :], preferred_element_type=jnp.float32)
    lagged += jnp.dot(lt_ref[:, span:], xs[:span, :], preferred_element_type=jnp.float32)
    lag_ref[...] = lagged * scale_ref[0]


def chunk_call(base, steps, z, scale, st, lt, frames, received, outs):
    rows, total = st.shape
    depth, columns = frames.shape
    width = steps * BLOCK
    smem = pl.BlockSpec(memory_space=pltpu.SMEM)
    whole = lambda a: pl.BlockSpec(a.shape, lambda j: (0, 0), pipeline_mode=pl.Buffered(1))
    part = pl.BlockSpec((depth, BLOCK), lambda j: (0, j))
    out_spec = pl.BlockSpec((rows, BLOCK), lambda j: (0, base + j))
    shape = jax.ShapeDtypeStruct((rows, columns), jnp.float32)
    operands = [z, scale, st, lt, frames, *received, *outs]
    specs = [smem, smem, whole(st), whole(lt), pl.BlockSpec((depth, BLOCK), lambda j: (0, base + j))]
    specs += [part] * len(received) + [pl.BlockSpec(memory_space=pl.ANY)] * len(outs)
    first = len(operands) - len(outs)
    flops = 2 * rows * width * (total + 2 * (total - LAG))
    return pl.pallas_call(
        functools.partial(chunk_kernel, total),
        out_shape=(shape, shape),
        grid=(steps,),
        in_specs=specs,
        out_specs=(out_spec, out_spec),
        scratch_shapes=[pltpu.VMEM((total, BLOCK), jnp.bfloat16)],
        input_output_aliases={first + k: k for k in range(len(outs))},
        cost_estimate=pl.CostEstimate(flops=flops, bytes_accessed=8 * rows * width + 5 * 2**20, transcendentals=0),
        compiler_params=pltpu.CompilerParams(vmem_limit_bytes=24 * 2**20),
    )(*operands)


def spread(value, axis):
    return lax.all_to_all(value, axis, split_axis=0, concat_axis=0, tiled=False)


def slab_rows(frames, start):
    depth, columns = frames.shape
    tiles, times = lax.axis_size("tile"), lax.axis_size("tm")
    piece = S // tiles // times
    at = jnp.clip(start - lax.axis_index("tile") * columns + S, 0, columns + S)
    padded = jnp.pad(frames, ((0, 0), (S, S)))
    mine = lax.dynamic_slice_in_dim(padded, at, S, 1)
    mine = mine.reshape(depth, times, tiles, piece).transpose(2, 1, 0, 3)
    mine = spread(mine, "tile")
    mine = jnp.sum(mine.astype(jnp.float32), axis=0).astype(jnp.bfloat16)
    z = lax.axis_index("tm")
    kept = [lax.dynamic_index_in_dim(mine, z, 0, keepdims=False)]
    for k in range(1, times):
        away = lax.dynamic_index_in_dim(mine, jnp.bitwise_xor(z, k), 0, keepdims=False)
        kept.append(permute(away, [(a, a ^ k) for a in range(times)]))
    mine = jnp.zeros((times, depth, piece), jnp.bfloat16)
    for k, block in enumerate(kept):
        mine = lax.dynamic_update_index_in_dim(mine, block, jnp.bitwise_xor(z, k), 0)
    values = mine.reshape(times * depth, piece).astype(jnp.float32)
    mean = jnp.sum(values, axis=0) / (times * depth)
    centered = (values - mean).astype(jnp.bfloat16).T
    every = jnp.broadcast_to(centered[None], (tiles, piece, times * depth))
    return spread(every, "tile").reshape(S // times, times * depth)


def chunk_units(columns):
    units = columns // BLOCK
    if units == sum(UNITS):
        return UNITS
    return (units - units // 3, units // 3) if units >= 3 else (units,)


def permute(value, pairs):
    return lax.ppermute(value, "tm", pairs)


def shards(frames, segments, offset):
    columns = frames.shape[1]
    total = segments.shape[0]
    z = lax.axis_index("tm").astype(jnp.int32).reshape(1)
    span = total - LAG
    received = []
    first = 0
    for units in chunk_units(columns):
        own = frames[:, first * BLOCK:(first + units) * BLOCK]
        far = permute(own, [(0, 2), (2, 0), (1, 3), (3, 1)])
        near = permute(own, [(0, 1), (1, 0), (2, 3), (3, 2)])
        inner = permute(own, [(1, 2), (2, 1)])
        outer = permute(far, [(1, 0), (2, 3)])
        received.append((first, units, (near, far, inner, outer)))
        first += units
    st = slab_rows(frames, offset[0])
    valid = (segments[:span] == segments[LAG:]).astype(jnp.bfloat16)
    pairs = jnp.sum(valid.astype(jnp.float32))
    lt = jnp.concatenate([st[:, :span] * valid, st[:, LAG:] * valid], axis=1)
    scale = (0.5 / pairs).reshape(1)
    outs = ()
    for first, units, parts in received:
        outs = chunk_call(first, units, z, scale, st, lt, frames, parts, outs)
    return tuple(outs)


def solution(mesh):
    in_specs = (P("tm", "tile"), P(), P())
    out_specs = (P("tm", "tile"), P("tm", "tile"))
    return jax.shard_map(shards, mesh=mesh, in_specs=in_specs, out_specs=out_specs, check_vma=False)
```

time: 358 us -> 287 us (0.80)
  waiting for transfers between devices: 244 us -> 147 us
  Pallas kernels: 0 us -> 57.3 us
  starting transfers between devices: 4.79 us -> 56.9 us
  matrix products: 46.2 us -> 0 us
  other arithmetic: 34.7 us -> 4.32 us
  between operations: 16.2 us -> 2.22 us
  local copies, waits for them, and re-layouts: 11.4 us -> 18.4 us
    ppermute x0 -> x23, waiting for transfers between devices: none -> 120 us  [permute(): return lax.ppermute(value, 'tm', pairs)]
    psum x1 -> x0, waiting for transfers between devices: 106 us -> none  [broadcast(): return lax.psum(jnp.where(mine, value, jnp.zeros_like(value)), axis)]
    all_to_all x1 -> x2, waiting for transfers between devices: 105 us -> 26.6 us  [spread(): return lax.all_to_all(value, axis, split_axis=0, concat_axis=0, tiled=False)]
    pallas_call x0 -> x5, Pallas kernels: none -> 57.3 us  [chunk_call(): pl.pallas_call(functools.partial(chunk_kernel, total), out_shape=(shape,...]
    ppermute x0 -> x23, starting transfers between devices: none -> 47.2 us  [permute(): return lax.ppermute(value, 'tm', pairs)]
    dot_general x2 -> x0, matrix products: 46.2 us -> none  [the longest x1 27.8 us: shards(): lax.dot_general(left, right, dims, preferred_element_type=jnp.float32) * 0.5]
    all_gather x1 -> x0, waiting for transfers between devices: 32.4 us -> none  [shards(): all_columns = lax.all_gather(frames, 'tm', axis=0, tiled=True)]
    convert_element_type x3 -> x1, other arithmetic: 12.7 us -> 0.06 us  [slab_rows(): centered = (values - mean).astype(jnp.bfloat16).T]
  transfers between devices with their start and end apart: 3 -> 25, of which waited for: 3 -> 8; matrix products, arithmetic and copies ran while one was open for 5% -> 2% of each run, Pallas kernels for 0% -> 18%
where the time goes in v1:
time: 287 us; the launch traced here: 286 us
  waiting for transfers between devices  147 us (51%)
  Pallas kernels  57.3 us (20%)
  starting transfers between devices  56.9 us (20%)
  local copies, waits for them, and re-layouts  18.4 us (6%)
  other arithmetic  4.32 us (2%)
    ppermute x23, waiting for transfers between devices, permute(): return lax.ppermute(value, 'tm', pairs)  120 us
    pallas_call x5, Pallas kernels, chunk_call(): pl.pallas_call(functools.partial(chunk_kernel, total), out_shape=(shape,...  57.3 us
    ppermute x23, starting transfers between devices, permute(): return lax.ppermute(value, 'tm', pairs)  47.2 us
    all_to_all x2, waiting for transfers between devices, spread(): return lax.all_to_all(value, axis, split_axis=0, concat_axis=0, tiled=False)  26.6 us
    all_to_all x2, starting transfers between devices, spread(): return lax.all_to_all(value, axis, split_axis=0, concat_axis=0, tiled=False)  9.68 us
  transfers between devices with their start and end apart: 25, of which 8 were waited for; matrix products, arithmetic and copies ran while one was open for 2% of the time, Pallas kernels for 18%

profile of v1, /device:TPU:0, one launch (start us, length us, event | category | flops | bytes accessed | tf_op | source)
XLA Modules:
  0.0 285.9 jit_solution(17795565896361245037)
XLA Ops:
  1.3 3.2 %copy.17 = bf16[256,6144]{0,1:T(8,128)(2,1)S(1)} copy(bf16[256,6144]{1,0:T(8,128)(2,1)} %own_ref.9) | data formatting | bytes 6291456 | tf_op args[0]
  4.5 4.6 %pad_dynamic-slice_fusion = bf16[256,4096]{0,1:T(8,128)(2,1)} fusion(s32[]{:T(128)S(6)} %min.4, bf16[256,6144]{0,1:T(8,128)(2,1)S(1)} %copy.17), kind=kLoop, calls=%fused_computation | loop fusion | bytes 5242884 | tf_op jit(solution)/shard_map/dynamic_slice | solution.py:72
  9.1 4.2 %copy.18 = bf16[8,4,256,128]{3,1,2,0:T(4,128)(2,1)} copy(bf16[8,4,256,128]{2,3,0,1:T(8,128)(2,1)} %bitcast.28) | data formatting | bytes 4194304 | tf_op jit(solution)/shard_map/transpose | solution.py:73
  13.3 5.2 %all-to-all-start = ((bf16[8,4,256,128]{3,1,2,0:T(4,128)(2,1)}), bf16[8,4,256,128]{3,1,2,0:T(4,128)(2,1)S(1)}, u32[]{:S(2)}, u32[]{:S(2)}) async-start(bf16[8,4,256,128]{3,1,2,0:T(4,128)(2,1)} %copy.18), calls=%async_computation | async-start | bytes 4194304 | tf_op jit(solution)/shard_map/all_to_all | solution.py:63
  18.5 26.6 %all-to-all-done = bf16[8,4,256,128]{3,1,2,0:T(4,128)(2,1)S(1)} async-done(((bf16[8,4,256,128]{3,1,2,0:T(4,128)(2,1)}), bf16[8,4,256,128]{3,1,2,0:T(4,128)(2,1)S(1)}, u32[]{:S(2)}, u32[]{:S(2)}) %all-to-all-start) | async-done | bytes 2097184 | tf_op jit(solution)/shard_map/all_to_all | solution.py:63
  45.1 1.2 reduce_sum.31
  46.3 0.6 constant_dynamic-slice_fusion
  46.9 1.6 collective-permute-start
  48.5 2.7 collective-permute-start.1
  51.2 0.3 collective-permute-start.2
  51.6 3.0 %collective-permute-done.1 = bf16[256,128]{1,0:T(8,128)(2,1)S(1)} collective-permute-done((bf16[256,128]{1,0:T(8,128)(2,1)S(1)}, bf16[256,128]{1,0:T(8,128)(2,1)S(1)}, u32[]{:S(2)}, u32[]{:S(2)}) %collective-permute-start.1) | collective-permute-done | bytes 65568 | tf_op jit(solution)/shard_map/ppermute | solution.py:99
  54.6 2.8 collective-permute-done.2
  57.7 1.6 broadcast_in_dim.27
  59.3 4.5 %all-to-all-start.1 = ((bf16[8,128,1024]{2,1,0:T(8,128)(2,1)}), bf16[8,128,1024]{2,1,0:T(8,128)(2,1)}, u32[]{:S(2)}, u32[]{:S(2)}) async-start(bf16[8,128,1024]{2,1,0:T(8,128)(2,1)} %broadcast_in_dim.27), calls=%async_computation.1 | async-start | bytes 4194304 | tf_op jit(solution)/shard_map/all_to_all | solution.py:63
  63.8 1.4 fusion.3
  65.3 1.2 collective-permute-start.19
  66.5 1.6 collective-permute-start.16
  68.1 1.6 collective-permute-start.21
  69.7 37.8 %collective-permute-done.20.far_ref = bf16[256,1792]{1,0:T(8,128)(2,1)} collective-permute-done((bf16[256,1792]{1,0:T(8,128)(2,1)}, bf16[256,1792]{1,0:T(8,128)(2,1)}, u32[]{:S(2)}, u32[]{:S(2)}) %collective-permute-start.20) | collective-permute-done | bytes 917536 | tf_op jit(solution)/shard_map/ppermute | solution.py:99
  107.5 1.3 collective-permute-start.22
  108.8 3.6 %collective-permute-start.15 = (bf16[256,1792]{1,0:T(8,128)(2,1)}, bf16[256,1792]{1,0:T(8,128)(2,1)}, u32[]{:S(2)}, u32[]{:S(2)}) collective-permute-start(bf16[256,1792]{1,0:T(8,128)(2,1)} %get-tuple-element.21), channel_id=1, source_target_pairs={{0,8},{8,0},{16,24},{24,16},{1,9},{9,1},{17,25},{25,17},{2,10},{10... | collective-permute-start | bytes 2752520 | tf_op jit(solution)/shard_map/ppermute | solution.py:99
  112.4 1.0 slice.33
  113.4 0.7 slice.31
  114.2 0.6 convert_reduce_fusion.1
  115.4 2.1 slice_multiply_fusion.1
  117.5 0.7 collective-permute-start.17
  118.2 28.0 %collective-permute-done.16.far_ref = bf16[256,1792]{1,0:T(8,128)(2,1)} collective-permute-done((bf16[256,1792]{1,0:T(8,128)(2,1)}, bf16[256,1792]{1,0:T(8,128)(2,1)}, u32[]{:S(2)}, u32[]{:S(2)}) %collective-permute-start.16) | collective-permute-done | bytes 917536 | tf_op jit(solution)/shard_map/ppermute | solution.py:99
  146.3 1.3 collective-permute-start.18
  147.8 0.8 copy-done.1
  148.6 19.5 %collective-permute-start.12 = (bf16[256,1280]{1,0:T(8,128)(2,1)S(1)}, bf16[256,1280]{1,0:T(8,128)(2,1)S(1)}, u32[]{:S(2)}, u32[]{:S(2)}) collective-permute-start(bf16[256,1280]{1,0:T(8,128)(2,1)S(1)} %copy-done.1), channel_id=1, source_target_pairs={{0,16},{16,0},{8,24},{24,8},{1,17},{17,1},{9,25},{25,9},{2,18},{18... | collective-permute-start | bytes 1966088 | tf_op jit(solution)/shard_map/ppermute | solution.py:99
  168.2 15.6 %shard_map.50 = (f32[1024,6144]{1,0:T(8,128)}, f32[1024,6144]{1,0:T(8,128)}) custom-call(s32[1]{0:T(128)} %bitcast.z_ref, f32[1]{0:T(128)} %bitcast.1.scale_ref, bf16[1024,1024]{1,0:T(8,128)(2,1)} %bitcast.10.st_ref, bf16[1024,1536]{1,0:T(8,128)(2,1)S(1)} %pad_maximum_fusion.lt_ref, bf16[256,6144]{1,0:T(8,128)(2,1)S(1)} %copy-done, ...), custom_call_target="tpu_custom_call" | custom-call | flops 9395240960 | bytes 19922944 | tf_op jit(solution)/shard_map/pallas_call | solution.py:49
  183.7 29.9 %collective-permute-done.12.far_ref = bf16[256,1280]{1,0:T(8,128)(2,1)S(1)} collective-permute-done((bf16[256,1280]{1,0:T(8,128)(2,1)S(1)}, bf16[256,1280]{1,0:T(8,128)(2,1)S(1)}, u32[]{:S(2)}, u32[]{:S(2)}) %collective-permute-start.12) | collective-permute-done | bytes 655392 | tf_op jit(solution)/shard_map/ppermute | solution.py:99
  213.6 0.7 collective-permute-start.13
  214.3 2.5 collective-permute-start.8
  216.8 0.8 collective-permute-start.7
  217.6 1.5 collective-permute-start.14
  219.1 15.6 %shard_map.51 = (f32[1024,6144]{1,0:T(8,128)}, f32[1024,6144]{1,0:T(8,128)}) custom-call(s32[1]{0:T(128)} %bitcast.z_ref, f32[1]{0:T(128)} %bitcast.1.scale_ref, bf16[1024,1024]{1,0:T(8,128)(2,1)} %bitcast.10.st_ref, bf16[1024,1536]{1,0:T(8,128)(2,1)S(1)} %pad_maximum_fusion.lt_ref, ...), custom_call_target="tpu_custom_call", output_to_operand_aliasing={{0}: (9, {}), {1}: (10, {})} | custom-call | flops 9395240960 | bytes 19922944 | tf_op jit(solution)/shard_map/pallas_call | solution.py:49
  234.6 13.2 %collective-permute-done.8.far_ref = bf16[256,768]{1,0:T(8,128)(2,1)S(1)} collective-permute-done((bf16[256,768]{1,0:T(8,128)(2,1)S(1)}, bf16[256,768]{1,0:T(8,128)(2,1)S(1)}, u32[]{:S(2)}, u32[]{:S(2)}) %collective-permute-start.8) | collective-permute-done | bytes 393248 | tf_op jit(solution)/shard_map/ppermute | solution.py:99
  247.8 0.7 collective-permute-start.9
  248.6 1.6 collective-permute-start.4
  250.1 0.8 collective-permute-start.3
  250.9 1.3 collective-permute-start.10
  252.2 11.8 %shard_map.52 = (f32[1024,6144]{1,0:T(8,128)}, f32[1024,6144]{1,0:T(8,128)}) custom-call(s32[1]{0:T(128)} %bitcast.z_ref, f32[1]{0:T(128)} %bitcast.1.scale_ref, bf16[1024,1024]{1,0:T(8,128)(2,1)} %bitcast.10.st_ref, bf16[1024,1536]{1,0:T(8,128)(2,1)S(1)} %pad_maximum_fusion.lt_ref, ...), custom_call_target="tpu_custom_call", output_to_operand_aliasing={{0}: (9, {}), {1}: (10, {})} | custom-call | flops 6710886400 | bytes 15728640 | tf_op jit(solution)/shard_map/pallas_call | solution.py:49
  263.9 5.6 %collective-permute-done.4.far_ref = bf16[256,512]{1,0:T(8,128)(2,1)S(1)} collective-permute-done((bf16[256,512]{1,0:T(8,128)(2,1)S(1)}, bf16[256,512]{1,0:T(8,128)(2,1)S(1)}, u32[]{:S(2)}, u32[]{:S(2)}) %collective-permute-start.4) | collective-permute-done | bytes 262176 | tf_op jit(solution)/shard_map/ppermute | solution.py:99
  269.5 0.7 collective-permute-start.5
  270.2 1.3 collective-permute-start.6
  271.5 8.1 %shard_map.53 = (f32[1024,6144]{1,0:T(8,128)}, f32[1024,6144]{1,0:T(8,128)}) custom-call(s32[1]{0:T(128)} %bitcast.z_ref, f32[1]{0:T(128)} %bitcast.1.scale_ref, bf16[1024,1024]{1,0:T(8,128)(2,1)} %bitcast.10.st_ref, bf16[1024,1536]{1,0:T(8,128)(2,1)S(1)} %pad_maximum_fusion.lt_ref, ...), custom_call_target="tpu_custom_call", output_to_operand_aliasing={{0}: (9, {}), {1}: (10, {})} | custom-call | flops 4026531840 | bytes 11534336 | tf_op jit(solution)/shard_map/pallas_call | solution.py:49
  279.7 6.3 %shard_map.54 = (f32[1024,6144]{1,0:T(8,128)}, f32[1024,6144]{1,0:T(8,128)}) custom-call(s32[1]{0:T(128)} %bitcast.z_ref, f32[1]{0:T(128)} %bitcast.1.scale_ref, bf16[1024,1024]{1,0:T(8,128)(2,1)} %bitcast.10.st_ref, bf16[1024,1536]{1,0:T(8,128)(2,1)S(1)} %pad_maximum_fusion.lt_ref, ...), custom_call_target="tpu_custom_call", output_to_operand_aliasing={{0}: (9, {}), {1}: (10, {})} | custom-call | flops 2684354560 | bytes 9437184 | tf_op jit(solution)/shard_map/pallas_call | solution.py:49
  (40 shorter events, 0.9 us)
Async XLA Ops:
  13.3 31.8 %all-to-all-start = ((bf16[8,4,256,128]{3,1,2,0:T(4,128)(2,1)}), bf16[8,4,256,128]{3,1,2,0:T(4,128)(2,1)S(1)}, u32[]{:S(2)}, u32[]{:S(2)}) async-start(bf16[8,4,256,128]{3,1,2,0:T(4,128)(2,1)} %copy.18), calls=%async_computation | async-start | bytes 4194304 | tf_op jit(solution)/shard_map/all_to_all | solution.py:63
  46.9 4.7 %collective-permute-start = (bf16[256,128]{1,0:T(8,128)(2,1)S(1)}, bf16[256,128]{1,0:T(8,128)(2,1)S(1)}, u32[]{:S(2)}, u32[]{:S(2)}) collective-permute-start(bf16[256,128]{1,0:T(8,128)(2,1)S(1)} %bitcast.32), channel_id=1, source_target_pairs={{0,8},{8,0},{16,24},{24,16},{1,9},{9,1},{17,25},{25,17},{2,10},{10... | collective-permute-start | bytes 196616 | tf_op jit(solution)/shard_map/ppermute | solution.py:99
  48.5 6.0 %collective-permute-start.1 = (bf16[256,128]{1,0:T(8,128)(2,1)S(1)}, bf16[256,128]{1,0:T(8,128)(2,1)S(1)}, u32[]{:S(2)}, u32[]{:S(2)}) collective-permute-start(bf16[256,128]{1,0:T(8,128)(2,1)S(1)} %bitcast.31), channel_id=1, source_target_pairs={{0,16},{8,24},{16,0},{24,8},{1,17},{9,25},{17,1},{25,9},{2,18},{10... | collective-permute-start | bytes 196616 | tf_op jit(solution)/shard_map/ppermute | solution.py:99
  51.2 6.1 %collective-permute-start.2 = (bf16[256,128]{1,0:T(8,128)(2,1)S(1)}, bf16[256,128]{1,0:T(8,128)(2,1)S(1)}, u32[]{:S(2)}, u32[]{:S(2)}) collective-permute-start(bf16[256,128]{1,0:T(8,128)(2,1)S(1)} %bitcast.30), channel_id=1, source_target_pairs={{0,24},{8,16},{16,8},{24,0},{1,25},{9,17},{17,9},{25,1},{2,26},{10... | collective-permute-start | bytes 196616 | tf_op jit(solution)/shard_map/ppermute | solution.py:99
  57.7 6.1 %copy-start = (bf16[256,6144]{1,0:T(8,128)(2,1)S(1)}, bf16[256,6144]{1,0:T(8,128)(2,1)}, u32[]{:S(2)}) copy-start(bf16[256,6144]{1,0:T(8,128)(2,1)} %own_ref.9) | copy-start | bytes 9437188
  59.3 56.1 %all-to-all-start.1 = ((bf16[8,128,1024]{2,1,0:T(8,128)(2,1)}), bf16[8,128,1024]{2,1,0:T(8,128)(2,1)}, u32[]{:S(2)}, u32[]{:S(2)}) async-start(bf16[8,128,1024]{2,1,0:T(8,128)(2,1)} %broadcast_in_dim.27), calls=%async_computation.1 | async-start | bytes 4194304 | tf_op jit(solution)/shard_map/all_to_all | solution.py:63
  63.8 50.3 %copy-start.3 = (s32[1024]{0:T(1024)S(1)}, s32[1024]{0:T(1024)}, u32[]{:S(2)}) copy-start(s32[1024]{0:T(1024)} %param.4) | copy-start | bytes 12292
  65.2 42.3 %collective-permute-start.20 = (bf16[256,1792]{1,0:T(8,128)(2,1)}, bf16[256,1792]{1,0:T(8,128)(2,1)}, u32[]{:S(2)}, u32[]{:S(2)}) collective-permute-start(bf16[256,1792]{1,0:T(8,128)(2,1)} %get-tuple-element.20), channel_id=1, source_target_pairs={{0,16},{16,0},{8,24},{24,8},{1,17},{17,1},{9,25},{25,9},{2,18},{18... | collective-permute-start | bytes 2752520 | tf_op jit(solution)/shard_map/ppermute | solution.py:99
  65.3 52.2 %collective-permute-start.19 = (bf16[256,1792]{1,0:T(8,128)(2,1)}, bf16[256,1792]{1,0:T(8,128)(2,1)}, u32[]{:S(2)}, u32[]{:S(2)}) collective-permute-start(bf16[256,1792]{1,0:T(8,128)(2,1)} %get-tuple-element.20), channel_id=1, source_target_pairs={{0,8},{8,0},{16,24},{24,16},{1,9},{9,1},{17,25},{25,17},{2,10},{10... | collective-permute-start | bytes 2752520 | tf_op jit(solution)/shard_map/ppermute | solution.py:99
  66.5 79.8 %collective-permute-start.16 = (bf16[256,1792]{1,0:T(8,128)(2,1)}, bf16[256,1792]{1,0:T(8,128)(2,1)}, u32[]{:S(2)}, u32[]{:S(2)}) collective-permute-start(bf16[256,1792]{1,0:T(8,128)(2,1)} %get-tuple-element.21), channel_id=1, source_target_pairs={{0,16},{16,0},{8,24},{24,8},{1,17},{17,1},{9,25},{25,9},{2,18},{18... | collective-permute-start | bytes 2752520 | tf_op jit(solution)/shard_map/ppermute | solution.py:99
  68.1 79.7 %collective-permute-start.21 = (bf16[256,1792]{1,0:T(8,128)(2,1)}, bf16[256,1792]{1,0:T(8,128)(2,1)}, u32[]{:S(2)}, u32[]{:S(2)}) collective-permute-start(bf16[256,1792]{1,0:T(8,128)(2,1)} %get-tuple-element.20), channel_id=1, source_target_pairs={{8,16},{16,8},{9,17},{17,9},{10,18},{18,10},{11,19},{19,11},{12,20... | collective-permute-start | bytes 2752520 | tf_op jit(solution)/shard_map/ppermute | solution.py:99
  107.5 60.7 %collective-permute-start.22 = (bf16[256,1792]{1,0:T(8,128)(2,1)}, bf16[256,1792]{1,0:T(8,128)(2,1)}, u32[]{:S(2)}, u32[]{:S(2)}) collective-permute-start(bf16[256,1792]{1,0:T(8,128)(2,1)} %collective-permute-done.20.far_ref), channel_id=1, source_target_pairs={{8,0},{16,24},{9,1},{17,25},{10,2},{18,26},{11,3},{19,27},{12,4},{... | collective-permute-start | bytes 2752520 | tf_op jit(solution)/shard_map/ppermute | solution.py:99
  108.8 105.5 %collective-permute-start.15 = (bf16[256,1792]{1,0:T(8,128)(2,1)}, bf16[256,1792]{1,0:T(8,128)(2,1)}, u32[]{:S(2)}, u32[]{:S(2)}) collective-permute-start(bf16[256,1792]{1,0:T(8,128)(2,1)} %get-tuple-element.21), channel_id=1, source_target_pairs={{0,8},{8,0},{16,24},{24,16},{1,9},{9,1},{17,25},{25,17},{2,10},{10... | collective-permute-start | bytes 2752520 | tf_op jit(solution)/shard_map/ppermute | solution.py:99
  117.5 99.3 %collective-permute-start.17 = (bf16[256,1792]{1,0:T(8,128)(2,1)}, bf16[256,1792]{1,0:T(8,128)(2,1)S(1)}, u32[]{:S(2)}, u32[]{:S(2)}) collective-permute-start(bf16[256,1792]{1,0:T(8,128)(2,1)} %get-tuple-element.21), channel_id=1, source_target_pairs={{8,16},{16,8},{9,17},{17,9},{10,18},{18,10},{11,19},{19,11},{12,20... | collective-permute-start | bytes 2752520 | tf_op jit(solution)/shard_map/ppermute | solution.py:99
  146.3 71.3 %collective-permute-start.18 = (bf16[256,1792]{1,0:T(8,128)(2,1)}, bf16[256,1792]{1,0:T(8,128)(2,1)S(1)}, u32[]{:S(2)}, u32[]{:S(2)}) collective-permute-start(bf16[256,1792]{1,0:T(8,128)(2,1)} %collective-permute-done.16.far_ref), channel_id=1, source_target_pairs={{8,0},{16,24},{9,1},{17,25},{10,2},{18,26},{11,3},{19,27},{12,4},{... | collective-permute-start | bytes 2752520 | tf_op jit(solution)/shard_map/ppermute | solution.py:99
  147.6 1.1 copy-start.1
  148.6 65.0 %collective-permute-start.12 = (bf16[256,1280]{1,0:T(8,128)(2,1)S(1)}, bf16[256,1280]{1,0:T(8,128)(2,1)S(1)}, u32[]{:S(2)}, u32[]{:S(2)}) collective-permute-start(bf16[256,1280]{1,0:T(8,128)(2,1)S(1)} %copy-done.1), channel_id=1, source_target_pairs={{0,16},{16,0},{8,24},{24,8},{1,17},{17,1},{9,25},{25,9},{2,18},{18... | collective-permute-start | bytes 1966088 | tf_op jit(solution)/shard_map/ppermute | solution.py:99
  168.2 80.4 %collective-permute-start.11 = (bf16[256,1280]{1,0:T(8,128)(2,1)S(1)}, bf16[256,1280]{1,0:T(8,128)(2,1)S(1)}, u32[]{:S(2)}, u32[]{:S(2)}) collective-permute-start(bf16[256,1280]{1,0:T(8,128)(2,1)S(1)} %copy-done.1), channel_id=1, source_target_pairs={{0,8},{8,0},{16,24},{24,16},{1,9},{9,1},{17,25},{25,17},{2,10},{10... | collective-permute-start | bytes 1966088 | tf_op jit(solution)/shard_map/ppermute | solution.py:99
  213.6 36.5 %collective-permute-start.13 = (bf16[256,1280]{1,0:T(8,128)(2,1)S(1)}, bf16[256,1280]{1,0:T(8,128)(2,1)S(1)}, u32[]{:S(2)}, u32[]{:S(2)}) collective-permute-start(bf16[256,1280]{1,0:T(8,128)(2,1)S(1)} %copy-done.1), channel_id=1, source_target_pairs={{8,16},{16,8},{9,17},{17,9},{10,18},{18,10},{11,19},{19,11},{12,20... | collective-permute-start | bytes 1966088 | tf_op jit(solution)/shard_map/ppermute | solution.py:99
  214.3 33.5 %collective-permute-start.8 = (bf16[256,768]{1,0:T(8,128)(2,1)S(1)}, bf16[256,768]{1,0:T(8,128)(2,1)S(1)}, u32[]{:S(2)}, u32[]{:S(2)}) collective-permute-start(bf16[256,768]{1,0:T(8,128)(2,1)S(1)} %slice.32), channel_id=1, source_target_pairs={{0,16},{16,0},{8,24},{24,8},{1,17},{17,1},{9,25},{25,9},{2,18},{18... | collective-permute-start | bytes 1179656 | tf_op jit(solution)/shard_map/ppermute | solution.py:99
  216.8 53.4 %collective-permute-start.7 = (bf16[256,768]{1,0:T(8,128)(2,1)S(1)}, bf16[256,768]{1,0:T(8,128)(2,1)S(1)}, u32[]{:S(2)}, u32[]{:S(2)}) collective-permute-start(bf16[256,768]{1,0:T(8,128)(2,1)S(1)} %slice.32), channel_id=1, source_target_pairs={{0,8},{8,0},{16,24},{24,16},{1,9},{9,1},{17,25},{25,17},{2,10},{10... | collective-permute-start | bytes 1179656 | tf_op jit(solution)/shard_map/ppermute | solution.py:99
  217.6 33.3 %collective-permute-start.14 = (bf16[256,1280]{1,0:T(8,128)(2,1)S(1)}, bf16[256,1280]{1,0:T(8,128)(2,1)S(1)}, u32[]{:S(2)}, u32[]{:S(2)}) collective-permute-start(bf16[256,1280]{1,0:T(8,128)(2,1)S(1)} %collective-permute-done.12.far_ref), channel_id=1, source_target_pairs={{8,0},{16,24},{9,1},{17,25},{10,2},{18,26},{11,3},{19,27},{12,4},{... | collective-permute-start | bytes 1966088 | tf_op jit(solution)/shard_map/ppermute | solution.py:99
  219.1 29.5 %copy-start.2 = (bf16[256,512]{1,0:T(8,128)(2,1)S(1)}, bf16[256,512]{1,0:T(8,128)(2,1)}, u32[]{:S(2)}) copy-start(bf16[256,512]{1,0:T(8,128)(2,1)} %slice.31) | copy-start | bytes 786436
  247.8 23.7 %collective-permute-start.9 = (bf16[256,768]{1,0:T(8,128)(2,1)S(1)}, bf16[256,768]{1,0:T(8,128)(2,1)S(1)}, u32[]{:S(2)}, u32[]{:S(2)}) collective-permute-start(bf16[256,768]{1,0:T(8,128)(2,1)S(1)} %slice.32), channel_id=1, source_target_pairs={{8,16},{16,8},{9,17},{17,9},{10,18},{18,10},{11,19},{19,11},{12,20... | collective-permute-start | bytes 1179656 | tf_op jit(solution)/shard_map/ppermute | solution.py:99
  248.6 21.0 %collective-permute-start.4 = (bf16[256,512]{1,0:T(8,128)(2,1)S(1)}, bf16[256,512]{1,0:T(8,128)(2,1)S(1)}, u32[]{:S(2)}, u32[]{:S(2)}) collective-permute-start(bf16[256,512]{1,0:T(8,128)(2,1)S(1)} %copy-done.2), channel_id=1, source_target_pairs={{0,16},{16,0},{8,24},{24,8},{1,17},{17,1},{9,25},{25,9},{2,18},{18... | collective-permute-start | bytes 786440 | tf_op jit(solution)/shard_map/ppermute | solution.py:99
  250.1 29.5 %collective-permute-start.3 = (bf16[256,512]{1,0:T(8,128)(2,1)S(1)}, bf16[256,512]{1,0:T(8,128)(2,1)S(1)}, u32[]{:S(2)}, u32[]{:S(2)}) collective-permute-start(bf16[256,512]{1,0:T(8,128)(2,1)S(1)} %copy-done.2), channel_id=1, source_target_pairs={{0,8},{8,0},{16,24},{24,16},{1,9},{9,1},{17,25},{25,17},{2,10},{10... | collective-permute-start | bytes 786440 | tf_op jit(solution)/shard_map/ppermute | solution.py:99
  250.9 20.6 %collective-permute-start.10 = (bf16[256,768]{1,0:T(8,128)(2,1)S(1)}, bf16[256,768]{1,0:T(8,128)(2,1)S(1)}, u32[]{:S(2)}, u32[]{:S(2)}) collective-permute-start(bf16[256,768]{1,0:T(8,128)(2,1)S(1)} %collective-permute-done.8.far_ref), channel_id=1, source_target_pairs={{8,0},{16,24},{9,1},{17,25},{10,2},{18,26},{11,3},{19,27},{12,4},{... | collective-permute-start | bytes 1179656 | tf_op jit(solution)/shard_map/ppermute | solution.py:99
  269.5 10.1 %collective-permute-start.5 = (bf16[256,512]{1,0:T(8,128)(2,1)S(1)}, bf16[256,512]{1,0:T(8,128)(2,1)S(1)}, u32[]{:S(2)}, u32[]{:S(2)}) collective-permute-start(bf16[256,512]{1,0:T(8,128)(2,1)S(1)} %copy-done.2), channel_id=1, source_target_pairs={{8,16},{16,8},{9,17},{17,9},{10,18},{18,10},{11,19},{19,11},{12,20... | collective-permute-start | bytes 786440 | tf_op jit(solution)/shard_map/ppermute | solution.py:99
  270.2 9.4 %collective-permute-start.6 = (bf16[256,512]{1,0:T(8,128)(2,1)S(1)}, bf16[256,512]{1,0:T(8,128)(2,1)S(1)}, u32[]{:S(2)}, u32[]{:S(2)}) collective-permute-start(bf16[256,512]{1,0:T(8,128)(2,1)S(1)} %collective-permute-done.4.far_ref), channel_id=1, source_target_pairs={{8,0},{16,24},{9,1},{17,25},{10,2},{18,26},{11,3},{19,27},{12,4},{... | collective-permute-start | bytes 786440 | tf_op jit(solution)/shard_map/ppermute | solution.py:99
